TPU v7x, 256 devices: a whole 4x4x8 slice. The times are simulated.
256 devices in a mesh: samples: 64 (over z, y, x_lo), vblocks: 4 (over x_hi, core).
Axes of the slice: x: 4 (x_hi: 2, x_lo: 2; x = x_hi * 2 + x_lo), y: 4, z: 8, core: 2. Of those that a mesh axis runs over, the one named last changes fastest.
Arguments:
- genotypes: int32 [65536, 4096], P('samples', 'vblocks'), may hold values from 0 to 2
- typed_mask: int32 [4096], P('vblocks'), may hold values 0 or 1
- z_scores: float32 [1024, 4096], P('samples', 'vblocks'), may hold values from -60 to 60
Outputs:
- solution: float32 [1024, 4096], P('samples', 'vblocks')
- imputed: float32 [1024, 4096], P('samples', 'vblocks')
All inputs are finite; a program needn't handle non-finite values. No bound on the sum of `typed_mask` on one device may be relied on, other than what follows from the above.
Results may differ from a plain program's by a relative error of at most 0.0068.
Values may be sent and summed in bfloat16 or wider, within the bound.
No kernel may reach another device: no remote copies, remote signals or barrier semaphores. Data moves between devices by JAX's collectives and lax.ppermute only.
A program may use at most 64 MiB of HBM per device.

v0:
```python
import jax
import jax.numpy as jnp
from jax import lax
from jax.sharding import Mesh, PartitionSpec as P

ITERS = 3
RIDGE = 0.1
EPSILON = 1e-05
HIGHEST = lax.Precision.HIGHEST
BF16 = jnp.bfloat16
F32 = jnp.float32
SAMPLE_AXES = ("z", "y", "xl")
BLOCK_AXES = ("xh", "core")
N_BLOCKS = 4


def from_next(block):
    return lax.ppermute(block, BLOCK_AXES, [(i + 1, i) for i in range(N_BLOCKS - 1)])


def from_previous(block):
    return lax.ppermute(block, BLOCK_AXES, [(i, i + 1) for i in range(N_BLOCKS - 1)])


def contract_rows(first_mat, second_mat):
    return lax.dot_general(
        first_mat, second_mat, (((0,), (0,)), ((), ())), preferred_element_type=F32
    )


def rounded(values):
    return lax.reduce_precision(values, exponent_bits=8, mantissa_bits=7)


def split3(vector):
    high = rounded(vector)
    rest = vector - high
    mid = rounded(rest)
    return jnp.concatenate([high, mid, rest - mid], axis=0).astype(BF16)


def join3(stacked):
    rows = stacked.shape[0] // 3
    return stacked[2 * rows :] + stacked[rows : 2 * rows] + stacked[:rows]


def times(vector, matrix, side):
    out = lax.dot_general(
        split3(vector), matrix, (((1,), (side,)), ((), ())), preferred_element_type=F32
    )
    return join3(out)


def gather_stats(local_sums, local_squares):
    sums, squares = (local_sums, local_squares)
    for axis in ("z", "y", "xl"):
        packed = jnp.concatenate([sums, squares], axis=0)[None]
        packed = lax.all_gather(packed, axis, axis=0, tiled=True)
        sums = packed[:, :-1].reshape(-1, packed.shape[-1])
        squares = jnp.sum(packed[:, -1], axis=0, keepdims=True)
    return (sums, squares)


def line_of(all_sums, all_squares, total_samples):
    coded_sum = jnp.sum(all_sums, axis=0, keepdims=True)
    mean_dosage = (coded_sum + total_samples) / total_samples
    squares = all_squares + 2.0 * coded_sum + total_samples
    variance = squares / total_samples - mean_dosage * mean_dosage
    scale = lax.rsqrt(variance + EPSILON)
    twos = 0.5 * (all_squares + coded_sum)
    zeros = 0.5 * (all_squares - coded_sum)
    ones = total_samples - all_squares
    level = rise = spread = 0.0
    for dosage, count in ((0.0, zeros), (1.0, ones), (2.0, twos)):
        away = dosage - mean_dosage
        value = rounded(away * scale)
        level = level + count * value
        rise = rise + count * value * away
        spread = spread + count * away * away
    slope = jnp.where(spread > 0.0, rise / jnp.where(spread > 0.0, spread, 1.0), scale)
    return (level / total_samples, slope)


def on_device(genotypes, typed_mask, z_scores):
    samples_dev, width = genotypes.shape
    n_dev = lax.axis_size(SAMPLE_AXES)
    total_samples = samples_dev * n_dev
    coded = (genotypes - 1).astype(BF16)
    following = from_next(coded)
    joined = jnp.concatenate([coded, following], axis=1)
    joined_f = joined.astype(F32)
    sums = jnp.sum(joined_f, axis=0, keepdims=True)
    squares = jnp.sum(joined_f * joined_f, axis=0, keepdims=True)
    counts = contract_rows(coded, joined)
    centred = (counts - sums[0, :width, None] * (sums / samples_dev)).astype(BF16)
    within = lax.psum_scatter(centred, "z", scatter_dimension=0, tiled=True)
    within = lax.psum_scatter(within.astype(F32), "y", scatter_dimension=0, tiled=True)
    within = lax.psum_scatter(within, "xl", scatter_dimension=0, tiled=True)
    all_sums, all_squares = gather_stats(sums, squares)
    level, slope = line_of(all_sums, all_squares, total_samples)
    off = (all_sums - jnp.mean(all_sums, axis=0, keepdims=True)) * slope
    rows = within.shape[0]
    start = lax.axis_index(SAMPLE_AXES) * rows
    off_rows = lax.dynamic_slice_in_dim(off, start, rows, axis=1)
    slope_rows = lax.dynamic_slice_in_dim(slope, start, rows, axis=1)
    level_rows = lax.dynamic_slice_in_dim(level, start, rows, axis=1)
    between = lax.dot_general(
        off_rows, off, (((0,), (0,)), ((), ())), precision=HIGHEST, preferred_element_type=F32
    )
    link = (within * slope * slope_rows[0][:, None] + between / samples_dev) / total_samples
    link = link + level_rows[0][:, None] * level
    link_rows = link.astype(BF16)
    gathered = lax.all_gather(link_rows, "xl", axis=0, tiled=True)
    gathered = lax.all_gather(gathered, "y", axis=0, tiled=True)
    gathered = lax.all_gather(gathered, "z", axis=0, tiled=True)
    own_block = gathered[:, :width]
    edge_block = gathered[:, width:]

    def apply_link(vector):
        ahead_part = from_next(vector)
        outgoing = times(vector, edge_block, 0)
        lower_part = from_previous(outgoing)
        result = times(vector, own_block, 1)
        result = result + 0.5 * times(ahead_part, edge_block, 1)
        return result + 0.5 * lower_part

    def dots(*pairs):
        local = jnp.stack([jnp.sum(a * b, axis=1) for a, b in pairs])
        return lax.psum(local, BLOCK_AXES)

    mask_row = typed_mask.astype(F32)[None, :]
    right_side = mask_row * z_scores
    residual = right_side
    linked = apply_link(mask_row * residual)
    image = mask_row * linked + RIDGE * residual
    norm_now, curvature = dots((residual, residual), (residual, image))
    direction = residual
    step_size = (norm_now / curvature)[:, None]
    solution = step_size * direction
    projected = step_size * linked
    for iteration in range(1, ITERS):
        residual = residual - step_size * image
        fresh_link = apply_link(mask_row * residual)
        fresh_image = mask_row * fresh_link + RIDGE * residual
        norm_next, fresh_curve, cross_a, cross_b, old_curve = dots(
            (residual, residual),
            (residual, fresh_image),
            (residual, image),
            (direction, fresh_image),
            (direction, image),
        )
        ratio = norm_next / norm_now
        curvature = fresh_curve + ratio * (cross_a + cross_b) + ratio * ratio * old_curve
        step_size = (norm_next / curvature)[:, None]
        direction = residual + ratio[:, None] * direction
        image = fresh_image + ratio[:, None] * image
        linked = fresh_link + ratio[:, None] * linked
        solution = solution + step_size * direction
        projected = projected + step_size * linked
        norm_now = norm_next
    imputed = jnp.where(typed_mask[None, :] == 1, z_scores, projected)
    return (solution, imputed)


def solution(mesh):
    fine = Mesh(mesh.devices.reshape(8, 4, 2, 2, 2), SAMPLE_AXES + BLOCK_AXES)
    placed = (P(SAMPLE_AXES, BLOCK_AXES), P(BLOCK_AXES), P(SAMPLE_AXES, BLOCK_AXES))
    return jax.shard_map(
        on_device,
        mesh=fine,
        in_specs=placed,
        out_specs=(P(SAMPLE_AXES, BLOCK_AXES), P(SAMPLE_AXES, BLOCK_AXES)),
        check_vma=False,
    )
```

profile of v0, /device:TPU:1, one launch (start us, length us, event | category | flops | bytes accessed | tf_op | source)
XLA Modules:
  0.0 291.5 jit_solution(16057749935253873127)
XLA Ops:
  7.2 2.8 add_convert_fusion
  10.0 5.1 %collective-permute-start = (bf16[1024,1024]{1,0:T(8,128)(2,1)S(1)}, bf16[1024,1024]{1,0:T(8,128)(2,1)S(1)}, u32[]{:S(2)}, u32[]{:S(2)}) collective-permute-start(bf16[1024,1024]{1,0:T(8,128)(2,1)S(1)} %add_convert_fusion), channel_id=1, source_target_pairs={{1,0},{2,1},{3,2},{5,4},{6,5},{7,6},{9,8},{10,9},{11,10},{13,12},{... | collective-permute-start | bytes 6291464 | tf_op jit(solution)/shard_map/ppermute | solution.py:18
  15.1 24.6 %collective-permute-done = bf16[1024,1024]{1,0:T(8,128)(2,1)S(1)} collective-permute-done((bf16[1024,1024]{1,0:T(8,128)(2,1)S(1)}, bf16[1024,1024]{1,0:T(8,128)(2,1)S(1)}, u32[]{:S(2)}, u32[]{:S(2)}) %collective-permute-start) | collective-permute-done | bytes 2097184 | tf_op jit(solution)/shard_map/ppermute | solution.py:18
  39.7 1.4 convert_reduce_fusion
  41.1 6.5 %subtract_convert_fusion = bf16[1024,2048]{1,0:T(8,128)(2,1)} fusion(f32[2048]{0:T(1024)S(1)} %broadcast_multiply_fusion.3, f32[1024]{0:T(1024)S(1)} %bitcast.95, bf16[1024,1024]{1,0:T(8,128)(2,1)S(1)} %add_convert_fusion, bf16[1024,1024]{1,0:T(8,128)(2,1)S(1)} %collective-permute-done), kind=kOutput, calls=%fused_computation.3 | convolution fusion | flops 4309647360 | bytes 8400896 | tf_op jit(solution)/shard_map/dot_general | solution.py:26
  47.7 23.4 %all-gather.3 = f32[8,2,2048]{2,1,0:T(2,128)S(1)} all-gather(f32[1,2,2048]{2,1,0:T(2,128)S(1)} %maximum_bitcast_fusion.2), channel_id=2, replica_groups=mesh['z'=8,'y'=4,'xl'=2,'xh'=2,'core'=2] {'z'}, dimensions={0}, use_global_device_ids=true | all-gather | bytes 147456 | tf_op jit(solution)/shard_map/all_gather | solution.py:58
  71.3 11.7 %all-gather.4 = f32[4,9,2048]{2,1,0:T(8,128)S(1)} all-gather(f32[1,9,2048]{2,1,0:T(8,128)S(1)} %maximum_bitcast_fusion.1), channel_id=3, replica_groups=mesh['z'=8,'y'=4,'xl'=2,'xh'=2,'core'=2] {'y'}, dimensions={0}, use_global_device_ids=true | all-gather | bytes 368640 | tf_op jit(solution)/shard_map/all_gather | solution.py:58
  83.0 21.1 %reduce-scatter.4.cloned.1.call-done = bf16[128,2048]{1,0:T(8,128)(2,1)} async-done(((bf16[1024,2048]{1,0:T(8,128)(2,1)}), bf16[128,2048]{1,0:T(8,128)(2,1)}) %reduce-scatter.4.cloned.1.call-update) | async-done | bytes 524304 | tf_op jit(solution)/shard_map/reduce_scatter | solution.py:96
  104.1 2.1 convert_element_type.31
  106.4 9.2 %all-gather.5 = f32[2,33,2048]{2,1,0:T(8,128)S(1)} all-gather(f32[1,33,2048]{2,1,0:T(8,128)S(1)} %maximum_bitcast_fusion), channel_id=4, replica_groups=mesh['z'=8,'y'=4,'xl'=2,'xh'=2,'core'=2] {'xl'}, dimensions={0}, use_global_device_ids=true | all-gather | bytes 811008 | tf_op jit(solution)/shard_map/all_gather | solution.py:58
  115.9 14.4 %reduce-scatter.6.cloned.1.call-done = f32[32,2048]{1,0:T(8,128)} async-done(((f32[128,2048]{1,0:T(8,128)}), f32[32,2048]{1,0:T(8,128)}) %reduce-scatter.6.cloned.1.call-update) | async-done | bytes 262160 | tf_op jit(solution)/shard_map/reduce_scatter | solution.py:97
  130.5 20.2 %reduce-scatter.8.cloned.1.call-done = f32[16,2048]{1,0:T(8,128)} async-done(((f32[32,2048]{1,0:T(8,128)}), f32[16,2048]{1,0:T(8,128)}) %reduce-scatter.8.cloned.1.call-update) | async-done | bytes 131088 | tf_op jit(solution)/shard_map/reduce_scatter | solution.py:98
  150.6 1.4 fusion.4
  152.0 3.8 %all_gather.21 = bf16[32,2048]{1,0:T(8,128)(2,1)S(1)} all-gather(bf16[16,2048]{1,0:T(8,128)(2,1)S(1)} %fusion.4), channel_id=1, replica_groups=mesh['z'=8,'y'=4,'xl'=2,'xh'=2,'core'=2] {'xl'}, dimensions={0}, use_global_device_ids=true | all-gather | bytes 196608 | tf_op jit(solution)/shard_map/all_gather | solution.py:113
  155.8 11.5 %all_gather.22 = bf16[128,2048]{1,0:T(8,128)(2,1)} all-gather(bf16[32,2048]{1,0:T(8,128)(2,1)S(1)} %all_gather.21), channel_id=1, replica_groups=mesh['z'=8,'y'=4,'xl'=2,'xh'=2,'core'=2] {'y'}, dimensions={0}, use_global_device_ids=true | all-gather | bytes 655360 | tf_op jit(solution)/shard_map/all_gather | solution.py:114
  167.3 6.7 %collective-permute-start.1 = (f32[16,1024]{1,0:T(8,128)S(1)}, f32[16,1024]{1,0:T(8,128)S(1)}, u32[]{:S(2)}, u32[]{:S(2)}) collective-permute-start(f32[16,1024]{1,0:T(8,128)S(1)} %get-tuple-element.28), channel_id=1, source_target_pairs={{1,0},{2,1},{3,2},{5,4},{6,5},{7,6},{9,8},{10,9},{11,10},{13,12},{... | collective-permute-start | bytes 196616 | tf_op jit(solution)/shard_map/ppermute | solution.py:18
  174.1 4.2 %collective-permute-done.1 = f32[16,1024]{1,0:T(8,128)S(1)} collective-permute-done((f32[16,1024]{1,0:T(8,128)S(1)}, f32[16,1024]{1,0:T(8,128)S(1)}, u32[]{:S(2)}, u32[]{:S(2)}) %collective-permute-start.1) | collective-permute-done | bytes 65568 | tf_op jit(solution)/shard_map/ppermute | solution.py:18
  178.3 48.0 %all-gather.8.cloned.1.call-done = bf16[1024,2048]{1,0:T(8,128)(2,1)} async-done(((bf16[128,2048]{1,0:T(8,128)(2,1)}), bf16[1024,2048]{1,0:T(8,128)(2,1)}) %all-gather.8.cloned.1.call-update) | async-done | bytes 4194320 | tf_op jit(solution)/shard_map/all_gather | solution.py:115
  226.3 2.2 fusion.19
  228.6 5.3 %collective-permute-start.2 = (f32[16,1024]{1,0:T(8,128)S(1)}, f32[16,1024]{1,0:T(8,128)S(1)}, u32[]{:S(2)}, u32[]{:S(2)}) collective-permute-start(f32[16,1024]{1,0:T(8,128)S(1)} %slice_add_fusion.12), channel_id=1, source_target_pairs={{0,1},{1,2},{2,3},{4,5},{5,6},{6,7},{8,9},{9,10},{10,11},{12,13},{... | collective-permute-start | bytes 196616 | tf_op jit(solution)/shard_map/ppermute | solution.py:22
  233.9 2.3 fusion.9
  237.2 6.6 %psum.21 = f32[2,16]{1,0:T(2,128)S(1)} all-reduce(f32[2,16]{1,0:T(2,128)S(1)} %pad_maximum_fusion.11), channel_id=1, replica_groups=mesh['z'=8,'y'=4,'xl'=2,'xh'=2,'core'=2] {'xh','core'}, use_global_device_ids=true, to_apply=%region_11.12 | all-reduce | flops 32 | bytes 256 | tf_op jit(solution)/shard_map/psum | solution.py:129
  244.0 3.2 %collective-permute-start.3 = (f32[16,1024]{1,0:T(8,128)S(1)}, f32[16,1024]{1,0:T(8,128)S(1)}, u32[]{:S(2)}, u32[]{:S(2)}) collective-permute-start(f32[16,1024]{1,0:T(8,128)S(1)} %get-tuple-element.25), channel_id=1, source_target_pairs={{1,0},{2,1},{3,2},{5,4},{6,5},{7,6},{9,8},{10,9},{11,10},{13,12},{... | collective-permute-start | bytes 196616 | tf_op jit(solution)/shard_map/ppermute | solution.py:18
  247.2 2.1 fusion.15
  249.3 4.7 %collective-permute-start.4 = (f32[16,1024]{1,0:T(8,128)S(1)}, f32[16,1024]{1,0:T(8,128)S(1)}, u32[]{:S(2)}, u32[]{:S(2)}) collective-permute-start(f32[16,1024]{1,0:T(8,128)S(1)} %slice_add_fusion.6), channel_id=1, source_target_pairs={{0,1},{1,2},{2,3},{4,5},{5,6},{6,7},{8,9},{9,10},{10,11},{12,13},{... | collective-permute-start | bytes 196616 | tf_op jit(solution)/shard_map/ppermute | solution.py:22
  253.9 2.3 fusion.7
  257.4 6.6 %psum.22 = f32[5,16]{1,0:T(8,128)S(1)} all-reduce(f32[5,16]{1,0:T(8,128)S(1)} %stack.50), channel_id=1, replica_groups=mesh['z'=8,'y'=4,'xl'=2,'xh'=2,'core'=2] {'xh','core'}, use_global_device_ids=true, to_apply=%region_16.17 | all-reduce | flops 80 | bytes 640 | tf_op jit(solution)/shard_map/psum | solution.py:129
  264.1 3.2 %collective-permute-start.5 = (f32[16,1024]{1,0:T(8,128)S(1)}, f32[16,1024]{1,0:T(8,128)S(1)}, u32[]{:S(2)}, u32[]{:S(2)}) collective-permute-start(f32[16,1024]{1,0:T(8,128)S(1)} %get-tuple-element.19), channel_id=1, source_target_pairs={{1,0},{2,1},{3,2},{5,4},{6,5},{7,6},{9,8},{10,9},{11,10},{13,12},{... | collective-permute-start | bytes 196616 | tf_op jit(solution)/shard_map/ppermute | solution.py:18
  267.4 2.1 fusion.11
  269.5 4.7 %collective-permute-start.6 = (f32[16,1024]{1,0:T(8,128)S(1)}, f32[16,1024]{1,0:T(8,128)S(1)}, u32[]{:S(2)}, u32[]{:S(2)}) collective-permute-start(f32[16,1024]{1,0:T(8,128)S(1)} %slice_add_fusion), channel_id=1, source_target_pairs={{0,1},{1,2},{2,3},{4,5},{5,6},{6,7},{8,9},{9,10},{10,11},{12,13},{... | collective-permute-start | bytes 196616 | tf_op jit(solution)/shard_map/ppermute | solution.py:22
  274.1 2.3 fusion.5
  277.6 6.6 %psum.23 = f32[5,16]{1,0:T(8,128)S(1)} all-reduce(f32[5,16]{1,0:T(8,128)S(1)} %stack.56), channel_id=1, replica_groups=mesh['z'=8,'y'=4,'xl'=2,'xh'=2,'core'=2] {'xh','core'}, use_global_device_ids=true, to_apply=%region_22.23 | all-reduce | flops 80 | bytes 640 | tf_op jit(solution)/shard_map/psum | solution.py:129
  (66 shorter events, 5.0 us)
Async XLA Ops:
  7.2 97.0 %reduce-scatter.4.cloned.1.call-start = ((), (), s32[]{:S(2)}) async-start(), calls=%async_computation.3 | async-start | bytes 4718592 | tf_op jit(solution)/shard_map/reduce_scatter | solution.py:96
  10.0 29.7 %collective-permute-start = (bf16[1024,1024]{1,0:T(8,128)(2,1)S(1)}, bf16[1024,1024]{1,0:T(8,128)(2,1)S(1)}, u32[]{:S(2)}, u32[]{:S(2)}) collective-permute-start(bf16[1024,1024]{1,0:T(8,128)(2,1)S(1)} %add_convert_fusion), channel_id=1, source_target_pairs={{1,0},{2,1},{3,2},{5,4},{6,5},{7,6},{9,8},{10,9},{11,10},{13,12},{... | collective-permute-start | bytes 6291464 | tf_op jit(solution)/shard_map/ppermute | solution.py:18
  47.6 82.6 %reduce-scatter.6.cloned.1.call-start = ((), (), s32[]{:S(2)}) async-start(), calls=%async_computation.4 | async-start | bytes 1310720 | tf_op jit(solution)/shard_map/reduce_scatter | solution.py:97
  106.3 61.0 %copy-start.1 = (s32[1024]{0:T(1024)S(1)}, s32[1024]{0:T(1024)}, u32[]{:S(2)}) copy-start(s32[1024]{0:T(1024)} %param.4) | copy-start | bytes 12292
  106.3 61.1 %copy-start = (f32[16,1024]{1,0:T(8,128)S(1)}, f32[16,1024]{1,0:T(8,128)}, u32[]{:S(2)}) copy-start(f32[16,1024]{1,0:T(8,128)} %param.5) | copy-start | bytes 196612
  106.3 44.3 %reduce-scatter.8.cloned.1.call-start = ((), (), s32[]{:S(2)}) async-start(), calls=%async_computation.5 | async-start | bytes 393216 | tf_op jit(solution)/shard_map/reduce_scatter | solution.py:98
  130.3 96.1 %all-gather.8.cloned.1.call-start = ((), (), s32[]{:S(2)}) async-start(), calls=%async_computation.6 | async-start | bytes 4718592 | tf_op jit(solution)/shard_map/all_gather | solution.py:115
  167.3 11.0 %collective-permute-start.1 = (f32[16,1024]{1,0:T(8,128)S(1)}, f32[16,1024]{1,0:T(8,128)S(1)}, u32[]{:S(2)}, u32[]{:S(2)}) collective-permute-start(f32[16,1024]{1,0:T(8,128)S(1)} %get-tuple-element.28), channel_id=1, source_target_pairs={{1,0},{2,1},{3,2},{5,4},{6,5},{7,6},{9,8},{10,9},{11,10},{13,12},{... | collective-permute-start | bytes 196616 | tf_op jit(solution)/shard_map/ppermute | solution.py:18
  226.3 9.9 %copy-start.2 = (bf16[1024,2048]{1,0:T(8,128)(2,1)S(1)}, bf16[1024,2048]{1,0:T(8,128)(2,1)}, u32[]{:S(2)}) copy-start(bf16[1024,2048]{1,0:T(8,128)(2,1)} %all-gather.8.cloned.1.call-done) | copy-start | bytes 12582916
  228.6 8.4 %collective-permute-start.2 = (f32[16,1024]{1,0:T(8,128)S(1)}, f32[16,1024]{1,0:T(8,128)S(1)}, u32[]{:S(2)}, u32[]{:S(2)}) collective-permute-start(f32[16,1024]{1,0:T(8,128)S(1)} %slice_add_fusion.12), channel_id=1, source_target_pairs={{0,1},{1,2},{2,3},{4,5},{5,6},{6,7},{8,9},{9,10},{10,11},{12,13},{... | collective-permute-start | bytes 196616 | tf_op jit(solution)/shard_map/ppermute | solution.py:22
  243.8 12.5 %copy-start.3 = (bf16[1024,2048]{1,0:T(8,128)(2,1)S(1)}, bf16[1024,2048]{1,0:T(8,128)(2,1)}, u32[]{:S(2)}) copy-start(bf16[1024,2048]{1,0:T(8,128)(2,1)} %all-gather.8.cloned.1.call-done) | copy-start | bytes 12582916
  244.0 12.3 %collective-permute-start.3 = (f32[16,1024]{1,0:T(8,128)S(1)}, f32[16,1024]{1,0:T(8,128)S(1)}, u32[]{:S(2)}, u32[]{:S(2)}) collective-permute-start(f32[16,1024]{1,0:T(8,128)S(1)} %get-tuple-element.25), channel_id=1, source_target_pairs={{1,0},{2,1},{3,2},{5,4},{6,5},{7,6},{9,8},{10,9},{11,10},{13,12},{... | collective-permute-start | bytes 196616 | tf_op jit(solution)/shard_map/ppermute | solution.py:18
  249.3 7.8 %collective-permute-start.4 = (f32[16,1024]{1,0:T(8,128)S(1)}, f32[16,1024]{1,0:T(8,128)S(1)}, u32[]{:S(2)}, u32[]{:S(2)}) collective-permute-start(f32[16,1024]{1,0:T(8,128)S(1)} %slice_add_fusion.6), channel_id=1, source_target_pairs={{0,1},{1,2},{2,3},{4,5},{5,6},{6,7},{8,9},{9,10},{10,11},{12,13},{... | collective-permute-start | bytes 196616 | tf_op jit(solution)/shard_map/ppermute | solution.py:22
  264.0 12.5 %copy-start.4 = (bf16[1024,2048]{1,0:T(8,128)(2,1)S(1)}, bf16[1024,2048]{1,0:T(8,128)(2,1)}, u32[]{:S(2)}) copy-start(bf16[1024,2048]{1,0:T(8,128)(2,1)} %all-gather.8.cloned.1.call-done) | copy-start | bytes 12582916
  264.1 12.3 %collective-permute-start.5 = (f32[16,1024]{1,0:T(8,128)S(1)}, f32[16,1024]{1,0:T(8,128)S(1)}, u32[]{:S(2)}, u32[]{:S(2)}) collective-permute-start(f32[16,1024]{1,0:T(8,128)S(1)} %get-tuple-element.19), channel_id=1, source_target_pairs={{1,0},{2,1},{3,2},{5,4},{6,5},{7,6},{9,8},{10,9},{11,10},{13,12},{... | collective-permute-start | bytes 196616 | tf_op jit(solution)/shard_map/ppermute | solution.py:18
  269.5 7.8 %collective-permute-start.6 = (f32[16,1024]{1,0:T(8,128)S(1)}, f32[16,1024]{1,0:T(8,128)S(1)}, u32[]{:S(2)}, u32[]{:S(2)}) collective-permute-start(f32[16,1024]{1,0:T(8,128)S(1)} %slice_add_fusion), channel_id=1, source_target_pairs={{0,1},{1,2},{2,3},{4,5},{5,6},{6,7},{8,9},{9,10},{10,11},{12,13},{... | collective-permute-start | bytes 196616 | tf_op jit(solution)/shard_map/ppermute | solution.py:22
Sparse Core Ops, SparseCore 0:
  47.7 56.3 reduce-scatter.3
  106.7 23.5 reduce-scatter.5
  132.7 17.8 reduce-scatter.7
  167.4 58.8 all-gather.7
where the time goes:
time: 292 us
  waiting for transfers between devices  133 us (46%)
  blocking collectives  79.5 us (27%)
  starting transfers between devices  33.1 us (11%)
  matrix products  23.4 us (8%)
  between operations  14.2 us (5%)
  other arithmetic  8.64 us (3%)
    all_gather x1, waiting for transfers between devices, on_device(): gathered = lax.all_gather(gathered, 'z', axis=0, tiled=True)  48 us
    all_gather x3, blocking collectives, gather_stats(): packed = lax.all_gather(packed, axis, axis=0, tiled=True)  44.3 us
    ppermute x4, waiting for transfers between devices, from_next(): lax.ppermute(block, BLOCK_AXES, [(i + 1, i) for i in range(N_BLOCKS - 1)])  28.8 us
    reduce_scatter x1, waiting for transfers between devices, on_device(): within = lax.psum_scatter(centred, 'z', scatter_dimension=0, tiled=True)  21.1 us
    reduce_scatter x1, waiting for transfers between devices, on_device(): within = lax.psum_scatter(within, 'xl', scatter_dimension=0, tiled=True)  20.2 us
    psum x3, blocking collectives, dots(): return lax.psum(local, BLOCK_AXES)  19.9 us
    ppermute x4, starting transfers between devices, from_next(): lax.ppermute(block, BLOCK_AXES, [(i + 1, i) for i in range(N_BLOCKS - 1)])  18.3 us
    dot_general x9, matrix products, times(): lax.dot_general(split3(vector), matrix, (((1,), (side,)), ((), ())), pref...  15.6 us
  transfers between devices with their start and end apart: 11, of which 6 were waited for; matrix products, arithmetic and copies ran while one was open for 5% of the time, Pallas kernels for 0%

commit v1 on v0

--- a/solution.py
+++ b/solution.py
@@ -126,7 +126,7 @@
 
     def dots(*pairs):
         local = jnp.stack([jnp.sum(a * b, axis=1) for a, b in pairs])
-        return lax.psum(local, BLOCK_AXES)
+        return lax.psum(lax.psum(local, "xh"), "core")
 
     mask_row = typed_mask.astype(F32)[None, :]
     right_side = mask_row * z_scores

time: 292 us -> 294 us (level)
  blocking collectives: 79.5 us -> 82.8 us
    psum x3 -> x6, blocking collectives: 19.9 us -> 23.2 us  [dots(): return lax.psum(lax.psum(local, 'xh'), 'core')]
where the time goes in v1:
time: 294 us
  waiting for transfers between devices  133 us (45%)
  blocking collectives  82.8 us (28%)
  starting transfers between devices  32 us (11%)
  matrix products  23.3 us (8%)
  between operations  14.2 us (5%)
  other arithmetic  8.61 us (3%)
    all_gather x1, waiting for transfers between devices, on_device(): gathered = lax.all_gather(gathered, 'z', axis=0, tiled=True)  48 us
    all_gather x3, blocking collectives, gather_stats(): packed = lax.all_gather(packed, axis, axis=0, tiled=True)  44.3 us
    ppermute x4, waiting for transfers between devices, from_next(): lax.ppermute(block, BLOCK_AXES, [(i + 1, i) for i in range(N_BLOCKS - 1)])  28.8 us
    psum x6, blocking collectives, dots(): return lax.psum(lax.psum(local, 'xh'), 'core')  23.2 us
    reduce_scatter x1, waiting for transfers between devices, on_device(): within = lax.psum_scatter(centred, 'z', scatter_dimension=0, tiled=True)  21.1 us
    reduce_scatter x1, waiting for transfers between devices, on_device(): within = lax.psum_scatter(within, 'xl', scatter_dimension=0, tiled=True)  20.2 us
    ppermute x4, starting transfers between devices, from_next(): lax.ppermute(block, BLOCK_AXES, [(i + 1, i) for i in range(N_BLOCKS - 1)])  16.5 us
    dot_general x9, matrix products, times(): lax.dot_general(split3(vector), matrix, (((1,), (side,)), ((), ())), pref...  15.6 us
  transfers between devices with their start and end apart: 11, of which 6 were waited for; matrix products, arithmetic and copies ran while one was open for 5% of the time, Pallas kernels for 0%

profile of v1, /device:TPU:1, one launch (start us, length us, event | category | flops | bytes accessed | tf_op | source)
XLA Modules:
  0.0 293.7 jit_solution(15815478988939840641)
XLA Ops:
  7.2 2.8 add_convert_fusion
  10.0 5.1 %collective-permute-start = (bf16[1024,1024]{1,0:T(8,128)(2,1)S(1)}, bf16[1024,1024]{1,0:T(8,128)(2,1)S(1)}, u32[]{:S(2)}, u32[]{:S(2)}) collective-permute-start(bf16[1024,1024]{1,0:T(8,128)(2,1)S(1)} %add_convert_fusion), channel_id=1, source_target_pairs={{1,0},{2,1},{3,2},{5,4},{6,5},{7,6},{9,8},{10,9},{11,10},{13,12},{... | collective-permute-start | bytes 6291464 | tf_op jit(solution)/shard_map/ppermute | solution.py:18
  15.1 24.6 %collective-permute-done = bf16[1024,1024]{1,0:T(8,128)(2,1)S(1)} collective-permute-done((bf16[1024,1024]{1,0:T(8,128)(2,1)S(1)}, bf16[1024,1024]{1,0:T(8,128)(2,1)S(1)}, u32[]{:S(2)}, u32[]{:S(2)}) %collective-permute-start) | collective-permute-done | bytes 2097184 | tf_op jit(solution)/shard_map/ppermute | solution.py:18
  41.1 6.4 %subtract_convert_fusion = bf16[1024,2048]{1,0:T(8,128)(2,1)} fusion(f32[2048]{0:T(1024)S(1)} %broadcast_multiply_fusion.3, f32[1024]{0:T(1024)S(1)} %bitcast.95, bf16[1024,1024]{1,0:T(8,128)(2,1)S(1)} %add_convert_fusion, bf16[1024,1024]{1,0:T(8,128)(2,1)S(1)} %collective-permute-done), kind=kOutput, calls=%fused_computation.3 | convolution fusion | flops 4309647360 | bytes 8400896 | tf_op jit(solution)/shard_map/dot_general | solution.py:26
  47.6 23.4 %all-gather.3 = f32[8,2,2048]{2,1,0:T(2,128)S(1)} all-gather(f32[1,2,2048]{2,1,0:T(2,128)S(1)} %maximum_bitcast_fusion.2), channel_id=2, replica_groups=mesh['z'=8,'y'=4,'xl'=2,'xh'=2,'core'=2] {'z'}, dimensions={0}, use_global_device_ids=true | all-gather | bytes 147456 | tf_op jit(solution)/shard_map/all_gather | solution.py:58
  71.2 11.7 %all-gather.4 = f32[4,9,2048]{2,1,0:T(8,128)S(1)} all-gather(f32[1,9,2048]{2,1,0:T(8,128)S(1)} %maximum_bitcast_fusion.1), channel_id=3, replica_groups=mesh['z'=8,'y'=4,'xl'=2,'xh'=2,'core'=2] {'y'}, dimensions={0}, use_global_device_ids=true | all-gather | bytes 368640 | tf_op jit(solution)/shard_map/all_gather | solution.py:58
  82.9 21.1 %reduce-scatter.4.cloned.1.call-done = bf16[128,2048]{1,0:T(8,128)(2,1)} async-done(((bf16[1024,2048]{1,0:T(8,128)(2,1)}), bf16[128,2048]{1,0:T(8,128)(2,1)}) %reduce-scatter.4.cloned.1.call-update) | async-done | bytes 524304 | tf_op jit(solution)/shard_map/reduce_scatter | solution.py:96
  104.0 2.1 convert_element_type.31
  106.3 9.2 %all-gather.5 = f32[2,33,2048]{2,1,0:T(8,128)S(1)} all-gather(f32[1,33,2048]{2,1,0:T(8,128)S(1)} %maximum_bitcast_fusion), channel_id=4, replica_groups=mesh['z'=8,'y'=4,'xl'=2,'xh'=2,'core'=2] {'xl'}, dimensions={0}, use_global_device_ids=true | all-gather | bytes 811008 | tf_op jit(solution)/shard_map/all_gather | solution.py:58
  115.7 14.4 %reduce-scatter.6.cloned.1.call-done = f32[32,2048]{1,0:T(8,128)} async-done(((f32[128,2048]{1,0:T(8,128)}), f32[32,2048]{1,0:T(8,128)}) %reduce-scatter.6.cloned.1.call-update) | async-done | bytes 262160 | tf_op jit(solution)/shard_map/reduce_scatter | solution.py:97
  130.3 20.2 %reduce-scatter.8.cloned.1.call-done = f32[16,2048]{1,0:T(8,128)} async-done(((f32[32,2048]{1,0:T(8,128)}), f32[16,2048]{1,0:T(8,128)}) %reduce-scatter.8.cloned.1.call-update) | async-done | bytes 131088 | tf_op jit(solution)/shard_map/reduce_scatter | solution.py:98
  151.9 3.8 %all_gather.21 = bf16[32,2048]{1,0:T(8,128)(2,1)S(1)} all-gather(bf16[16,2048]{1,0:T(8,128)(2,1)S(1)} %fusion.4), channel_id=1, replica_groups=mesh['z'=8,'y'=4,'xl'=2,'xh'=2,'core'=2] {'xl'}, dimensions={0}, use_global_device_ids=true | all-gather | bytes 196608 | tf_op jit(solution)/shard_map/all_gather | solution.py:113
  155.7 11.5 %all_gather.22 = bf16[128,2048]{1,0:T(8,128)(2,1)} all-gather(bf16[32,2048]{1,0:T(8,128)(2,1)S(1)} %all_gather.21), channel_id=1, replica_groups=mesh['z'=8,'y'=4,'xl'=2,'xh'=2,'core'=2] {'y'}, dimensions={0}, use_global_device_ids=true | all-gather | bytes 655360 | tf_op jit(solution)/shard_map/all_gather | solution.py:114
  167.3 6.7 %collective-permute-start.1 = (f32[16,1024]{1,0:T(8,128)S(1)}, f32[16,1024]{1,0:T(8,128)S(1)}, u32[]{:S(2)}, u32[]{:S(2)}) collective-permute-start(f32[16,1024]{1,0:T(8,128)S(1)} %get-tuple-element.28), channel_id=1, source_target_pairs={{1,0},{2,1},{3,2},{5,4},{6,5},{7,6},{9,8},{10,9},{11,10},{13,12},{... | collective-permute-start | bytes 196616 | tf_op jit(solution)/shard_map/ppermute | solution.py:18
  174.0 4.2 %collective-permute-done.1 = f32[16,1024]{1,0:T(8,128)S(1)} collective-permute-done((f32[16,1024]{1,0:T(8,128)S(1)}, f32[16,1024]{1,0:T(8,128)S(1)}, u32[]{:S(2)}, u32[]{:S(2)}) %collective-permute-start.1) | collective-permute-done | bytes 65568 | tf_op jit(solution)/shard_map/ppermute | solution.py:18
  178.3 48.0 %all-gather.8.cloned.1.call-done = bf16[1024,2048]{1,0:T(8,128)(2,1)} async-done(((bf16[128,2048]{1,0:T(8,128)(2,1)}), bf16[1024,2048]{1,0:T(8,128)(2,1)}) %all-gather.8.cloned.1.call-update) | async-done | bytes 4194320 | tf_op jit(solution)/shard_map/all_gather | solution.py:115
  226.3 2.2 fusion.19
  228.5 5.3 %collective-permute-start.2 = (f32[16,1024]{1,0:T(8,128)S(1)}, f32[16,1024]{1,0:T(8,128)S(1)}, u32[]{:S(2)}, u32[]{:S(2)}) collective-permute-start(f32[16,1024]{1,0:T(8,128)S(1)} %slice_add_fusion.12), channel_id=1, source_target_pairs={{0,1},{1,2},{2,3},{4,5},{5,6},{6,7},{8,9},{9,10},{10,11},{12,13},{... | collective-permute-start | bytes 196616 | tf_op jit(solution)/shard_map/ppermute | solution.py:22
  233.8 2.3 fusion.9
  237.1 5.3 %psum.42 = f32[2,16]{1,0:T(2,128)S(1)} all-reduce(f32[2,16]{1,0:T(2,128)S(1)} %pad_maximum_fusion.11), channel_id=1, replica_groups=mesh['z'=8,'y'=4,'xl'=2,'xh'=2,'core'=2] {'xh'}, use_global_device_ids=true, to_apply=%region_11.12 | all-reduce | flops 32 | bytes 256 | tf_op jit(solution)/shard_map/psum | solution.py:129
  242.4 2.5 psum.43
  245.0 2.3 collective-permute-start.3
  249.4 5.0 %collective-permute-start.4 = (f32[16,1024]{1,0:T(8,128)S(1)}, f32[16,1024]{1,0:T(8,128)S(1)}, u32[]{:S(2)}, u32[]{:S(2)}) collective-permute-start(f32[16,1024]{1,0:T(8,128)S(1)} %slice_add_fusion.6), channel_id=1, source_target_pairs={{0,1},{1,2},{2,3},{4,5},{5,6},{6,7},{8,9},{9,10},{10,11},{12,13},{... | collective-permute-start | bytes 196616 | tf_op jit(solution)/shard_map/ppermute | solution.py:22
  254.4 2.3 fusion.7
  257.8 5.3 %psum.44 = f32[5,16]{1,0:T(8,128)S(1)} all-reduce(f32[5,16]{1,0:T(8,128)S(1)} %stack.50), channel_id=1, replica_groups=mesh['z'=8,'y'=4,'xl'=2,'xh'=2,'core'=2] {'xh'}, use_global_device_ids=true, to_apply=%region_17.18 | all-reduce | flops 80 | bytes 640 | tf_op jit(solution)/shard_map/psum | solution.py:129
  263.1 2.5 psum.45
  265.7 2.3 collective-permute-start.5
  268.1 2.1 fusion.11
  270.2 5.0 %collective-permute-start.6 = (f32[16,1024]{1,0:T(8,128)S(1)}, f32[16,1024]{1,0:T(8,128)S(1)}, u32[]{:S(2)}, u32[]{:S(2)}) collective-permute-start(f32[16,1024]{1,0:T(8,128)S(1)} %slice_add_fusion), channel_id=1, source_target_pairs={{0,1},{1,2},{2,3},{4,5},{5,6},{6,7},{8,9},{9,10},{10,11},{12,13},{... | collective-permute-start | bytes 196616 | tf_op jit(solution)/shard_map/ppermute | solution.py:22
  275.2 2.3 fusion.5
  278.6 5.3 %psum.46 = f32[5,16]{1,0:T(8,128)S(1)} all-reduce(f32[5,16]{1,0:T(8,128)S(1)} %stack.56), channel_id=1, replica_groups=mesh['z'=8,'y'=4,'xl'=2,'xh'=2,'core'=2] {'xh'}, use_global_device_ids=true, to_apply=%region_24.25 | all-reduce | flops 80 | bytes 640 | tf_op jit(solution)/shard_map/psum | solution.py:129
  283.9 2.5 psum.47
  (69 shorter events, 9.7 us)
Async XLA Ops:
  7.2 96.8 %reduce-scatter.4.cloned.1.call-start = ((), (), s32[]{:S(2)}) async-start(), calls=%async_computation.3 | async-start | bytes 4718592 | tf_op jit(solution)/shard_map/reduce_scatter | solution.py:96
  10.0 29.7 %collective-permute-start = (bf16[1024,1024]{1,0:T(8,128)(2,1)S(1)}, bf16[1024,1024]{1,0:T(8,128)(2,1)S(1)}, u32[]{:S(2)}, u32[]{:S(2)}) collective-permute-start(bf16[1024,1024]{1,0:T(8,128)(2,1)S(1)} %add_convert_fusion), channel_id=1, source_target_pairs={{1,0},{2,1},{3,2},{5,4},{6,5},{7,6},{9,8},{10,9},{11,10},{13,12},{... | collective-permute-start | bytes 6291464 | tf_op jit(solution)/shard_map/ppermute | solution.py:18
  47.5 82.6 %reduce-scatter.6.cloned.1.call-start = ((), (), s32[]{:S(2)}) async-start(), calls=%async_computation.4 | async-start | bytes 1310720 | tf_op jit(solution)/shard_map/reduce_scatter | solution.py:97
  106.1 61.1 %copy-start.1 = (s32[1024]{0:T(1024)S(1)}, s32[1024]{0:T(1024)}, u32[]{:S(2)}) copy-start(s32[1024]{0:T(1024)} %param.4) | copy-start | bytes 12292
  106.1 61.1 %copy-start = (f32[16,1024]{1,0:T(8,128)S(1)}, f32[16,1024]{1,0:T(8,128)}, u32[]{:S(2)}) copy-start(f32[16,1024]{1,0:T(8,128)} %param.5) | copy-start | bytes 196612
  106.2 44.4 %reduce-scatter.8.cloned.1.call-start = ((), (), s32[]{:S(2)}) async-start(), calls=%async_computation.5 | async-start | bytes 393216 | tf_op jit(solution)/shard_map/reduce_scatter | solution.py:98
  130.1 96.1 %all-gather.8.cloned.1.call-start = ((), (), s32[]{:S(2)}) async-start(), calls=%async_computation.6 | async-start | bytes 4718592 | tf_op jit(solution)/shard_map/all_gather | solution.py:115
  167.3 11.0 %collective-permute-start.1 = (f32[16,1024]{1,0:T(8,128)S(1)}, f32[16,1024]{1,0:T(8,128)S(1)}, u32[]{:S(2)}, u32[]{:S(2)}) collective-permute-start(f32[16,1024]{1,0:T(8,128)S(1)} %get-tuple-element.28), channel_id=1, source_target_pairs={{1,0},{2,1},{3,2},{5,4},{6,5},{7,6},{9,8},{10,9},{11,10},{13,12},{... | collective-permute-start | bytes 196616 | tf_op jit(solution)/shard_map/ppermute | solution.py:18
  226.3 9.9 %copy-start.2 = (bf16[1024,2048]{1,0:T(8,128)(2,1)S(1)}, bf16[1024,2048]{1,0:T(8,128)(2,1)}, u32[]{:S(2)}) copy-start(bf16[1024,2048]{1,0:T(8,128)(2,1)} %all-gather.8.cloned.1.call-done) | copy-start | bytes 12582916
  228.5 8.4 %collective-permute-start.2 = (f32[16,1024]{1,0:T(8,128)S(1)}, f32[16,1024]{1,0:T(8,128)S(1)}, u32[]{:S(2)}, u32[]{:S(2)}) collective-permute-start(f32[16,1024]{1,0:T(8,128)S(1)} %slice_add_fusion.12), channel_id=1, source_target_pairs={{0,1},{1,2},{2,3},{4,5},{5,6},{6,7},{8,9},{9,10},{10,11},{12,13},{... | collective-permute-start | bytes 196616 | tf_op jit(solution)/shard_map/ppermute | solution.py:22
  244.9 11.9 %copy-start.3 = (bf16[1024,2048]{1,0:T(8,128)(2,1)S(1)}, bf16[1024,2048]{1,0:T(8,128)(2,1)}, u32[]{:S(2)}) copy-start(bf16[1024,2048]{1,0:T(8,128)(2,1)} %all-gather.8.cloned.1.call-done) | copy-start | bytes 12582916
  245.0 11.8 %collective-permute-start.3 = (f32[16,1024]{1,0:T(8,128)S(1)}, f32[16,1024]{1,0:T(8,128)S(1)}, u32[]{:S(2)}, u32[]{:S(2)}) collective-permute-start(f32[16,1024]{1,0:T(8,128)S(1)} %get-tuple-element.25), channel_id=1, source_target_pairs={{1,0},{2,1},{3,2},{5,4},{6,5},{7,6},{9,8},{10,9},{11,10},{13,12},{... | collective-permute-start | bytes 196616 | tf_op jit(solution)/shard_map/ppermute | solution.py:18
  249.4 8.1 %collective-permute-start.4 = (f32[16,1024]{1,0:T(8,128)S(1)}, f32[16,1024]{1,0:T(8,128)S(1)}, u32[]{:S(2)}, u32[]{:S(2)}) collective-permute-start(f32[16,1024]{1,0:T(8,128)S(1)} %slice_add_fusion.6), channel_id=1, source_target_pairs={{0,1},{1,2},{2,3},{4,5},{5,6},{6,7},{8,9},{9,10},{10,11},{12,13},{... | collective-permute-start | bytes 196616 | tf_op jit(solution)/shard_map/ppermute | solution.py:22
  265.6 12.0 %copy-start.4 = (bf16[1024,2048]{1,0:T(8,128)(2,1)S(1)}, bf16[1024,2048]{1,0:T(8,128)(2,1)}, u32[]{:S(2)}) copy-start(bf16[1024,2048]{1,0:T(8,128)(2,1)} %all-gather.8.cloned.1.call-done) | copy-start | bytes 12582916
  265.7 11.8 %collective-permute-start.5 = (f32[16,1024]{1,0:T(8,128)S(1)}, f32[16,1024]{1,0:T(8,128)S(1)}, u32[]{:S(2)}, u32[]{:S(2)}) collective-permute-start(f32[16,1024]{1,0:T(8,128)S(1)} %get-tuple-element.19), channel_id=1, source_target_pairs={{1,0},{2,1},{3,2},{5,4},{6,5},{7,6},{9,8},{10,9},{11,10},{13,12},{... | collective-permute-start | bytes 196616 | tf_op jit(solution)/shard_map/ppermute | solution.py:18
  270.2 8.1 %collective-permute-start.6 = (f32[16,1024]{1,0:T(8,128)S(1)}, f32[16,1024]{1,0:T(8,128)S(1)}, u32[]{:S(2)}, u32[]{:S(2)}) collective-permute-start(f32[16,1024]{1,0:T(8,128)S(1)} %slice_add_fusion), channel_id=1, source_target_pairs={{0,1},{1,2},{2,3},{4,5},{5,6},{6,7},{8,9},{9,10},{10,11},{12,13},{... | collective-permute-start | bytes 196616 | tf_op jit(solution)/shard_map/ppermute | solution.py:22
Sparse Core Ops, SparseCore 0:
  47.6 56.3 reduce-scatter.3
  106.6 23.4 reduce-scatter.5
  132.6 17.9 reduce-scatter.7
  167.3 58.8 all-gather.7
